TPU v7x, 32 devices: a whole 2x2x4 slice. The times are simulated.
32 devices in a mesh: slab: 2 (over y), bx: 8 (over z, x), by: 2 (over core).
Axes of the slice: x: 2, y: 2, z: 4, core: 2. Of those that a mesh axis runs over, the one named last changes fastest.
Arguments:
- phi: float32 [64, 128, 2048], P('slab', 'bx', 'by'), parts along dimension 0, may hold values from -6 to 6
- first_measurement: float32 [128, 2048], P('slab', 'by'), parts along dimension 0, may hold values from 0.5 to 3.5
- second_measurement: float32 [128, 128], P('slab', 'bx'), parts along dimension 0, may hold values from 0.5 to 3.5
- first_view_mask: int32 [128, 2048], P('slab', 'by'), parts along dimension 0, may hold values 0 or 1
- second_view_mask: int32 [128, 128], P('slab', 'bx'), parts along dimension 0, may hold values 0 or 1
- plane_detector_rows: int32 [32], replicated, may hold values from 0 to 63, as said below
Outputs:
- gradient: float32 [64, 128, 2048], P('slab', 'bx', 'by'), parts along dimension 0
There are 2 independent parts, one for each index of `slab`. A program takes and returns all parts, laid end to end along the dimension named above; an argument that names none is the same for every part. Nothing has to cross between parts.
Inputs may be any that keep to these rules, and one draw needn't show every extreme that they name: `plane_detector_rows`: plane z reads detector row 2 z or 2 z + 1; plane 0 reads row 0 and the last plane reads row 63.
All inputs are finite; a program needn't handle non-finite values. No bound on the sum of `first_view_mask` or of `second_view_mask` on one device may be relied on, other than what follows from the above.
Results may differ from a plain program's by a relative error of at most 0.00002.
Values sent between devices are 32-bit elements; how exact they have to be, the bound alone decides.
A program may use at most 64 MiB of HBM per device.

v0:
```python
import jax
import jax.numpy as jnp
from jax import lax
from jax.sharding import PartitionSpec as P

LAMBDA = 0.5
BETA2 = 1.0


def extended(cells, sides, width):
    for axis, dim in sides:
        count = lax.axis_size(axis)
        ends = count - 1
        head = lax.slice_in_dim(cells, 0, width, axis=dim)
        tail = lax.slice_in_dim(cells, cells.shape[dim] - width, cells.shape[dim], axis=dim)
        cells = jnp.concatenate(
            [
                lax.ppermute(tail, axis, [(i, (i + 1) % count) for i in range(ends)]),
                cells,
                lax.ppermute(head, axis, [((i + 1) % count, i) for i in range(ends)]),
            ],
            axis=dim,
        )
    return cells


def curvature_of(padded):
    core = padded[:-1, :-1, :-1]
    grad_z = padded[1:, :-1, :-1] - core
    grad_x = padded[:-1, 1:, :-1] - core
    grad_y = padded[:-1, :-1, 1:] - core
    magnitude = jnp.sqrt(grad_z * grad_z + grad_x * grad_x + grad_y * grad_y + BETA2)
    flux_z = grad_z / magnitude
    flux_x = grad_x / magnitude
    flux_y = grad_y / magnitude
    div_z = flux_z[1:, 1:, 1:] - flux_z[:-1, 1:, 1:]
    div_x = flux_x[1:, 1:, 1:] - flux_x[1:, :-1, 1:]
    div_y = flux_y[1:, 1:, 1:] - flux_y[1:, 1:, :-1]
    return div_z + div_x + div_y


def per_device(
    phi,
    first_measurement,
    second_measurement,
    first_view_mask,
    second_view_mask,
    plane_detector_rows,
):
    planes, cells_x, cells_y = phi.shape
    total_x = cells_x * lax.axis_size("bx")
    total_y = cells_y * lax.axis_size("by")
    tanh_phi = jnp.tanh(phi)
    heav = 0.5 * (1.0 + tanh_phi)
    slope = 0.5 * (1.0 - tanh_phi * tanh_phi)
    part_a = jnp.sum(heav, axis=1)
    part_b = jnp.sum(heav, axis=2)
    first_measured_rows = jnp.take(first_measurement, plane_detector_rows, axis=0)
    first_mask_rows = jnp.take(first_view_mask, plane_detector_rows, axis=0).astype(jnp.float32)
    second_measured_rows = jnp.take(second_measurement, plane_detector_rows, axis=0)
    second_mask_rows = jnp.take(second_view_mask, plane_detector_rows, axis=0).astype(jnp.float32)
    second_projection = lax.psum(part_b, "by") * (4.0 / total_y)
    second_residual = second_mask_rows * (second_projection - second_measured_rows)
    first_projection = lax.psum(part_a, "bx") * (4.0 / total_x)
    first_residual = first_mask_rows * (first_projection - first_measured_rows)
    padded = extended(phi, (("bx", 1), ("by", 2)), 1)
    padded = jnp.pad(padded, ((1, 1), (0, 0), (0, 0)))
    curv = curvature_of(padded)
    return slope * (first_residual[:, None, :] + second_residual[:, :, None]) - LAMBDA * curv


def solution(mesh):
    in_specs = (
        P("slab", "bx", "by"),
        P("slab", "by"),
        P("slab", "bx"),
        P("slab", "by"),
        P("slab", "bx"),
        P(),
    )
    out_specs = P("slab", "bx", "by")
    return jax.shard_map(
        per_device, mesh=mesh, in_specs=in_specs, out_specs=out_specs, check_vma=False
    )
```

profile of v0, /device:TPU:0, one launch (start us, length us, event | category | flops | bytes accessed | tf_op | source)
XLA Modules:
  0.0 121.4 jit_solution(6646163909018269001)
XLA Ops:
  6.5 0.0 all-reduce.3.cloned.1.call-start
  6.6 1.9 %fusion.10 = (f32[32,1,1024]{2,1,0:T(1,128)S(1)}, f32[32,1,1024]{2,1,0:T(1,128)S(1)}) fusion(f32[32,16,1024]{2,1,0:T(8,128)} %param.6), kind=kLoop, calls=%fused_computation.29 | loop fusion | bytes 524288 | tf_op jit(solution)/shard_map/slice | solution.py:15
  8.5 4.9 %collective-permute-start = (f32[32,1,1024]{2,0,1:T(8,128)S(1)}, f32[32,1,1024]{2,0,1:T(8,128)S(1)}, u32[]{:S(2)}, u32[]{:S(2)}) collective-permute-start(f32[32,1,1024]{2,0,1:T(8,128)S(1)} %copy.15), channel_id=1, source_target_pairs={{0,2},{2,4},{4,6},{6,8},{8,10},{10,12},{12,14},{1,3},{3,5},{5,7},{... | collective-permute-start | bytes 393224 | tf_op jit(solution)/shard_map/ppermute | solution.py:18
  13.5 1.3 %collective-permute-start.1 = (f32[32,1,1024]{2,0,1:T(8,128)S(1)}, f32[32,1,1024]{2,0,1:T(8,128)S(1)}, u32[]{:S(2)}, u32[]{:S(2)}) collective-permute-start(f32[32,1,1024]{2,0,1:T(8,128)S(1)} %copy.16), channel_id=1, source_target_pairs={{2,0},{4,2},{6,4},{8,6},{10,8},{12,10},{14,12},{3,1},{5,3},{7,5},{... | collective-permute-start | bytes 393224 | tf_op jit(solution)/shard_map/ppermute | solution.py:20
  14.8 2.9 %fusion.5 = (f32[32,1024]{1,0:T(8,128)}, f32[32,16]{1,0:T(8,128)S(1)}) fusion(f32[32,16,1024]{2,1,0:T(8,128)} %param.6), kind=kLoop, calls=%fused_computation.19 | loop fusion | flops 2063872 | bytes 2230272 | tf_op jit(solution)/shard_map/reduce_sum | solution.py:56
  17.7 0.0 all-reduce.3.cloned.1.call-update
  17.7 0.7 compare_select_fusion
  18.4 0.7 compare_and_fusion
  19.0 0.6 gather_fusion
  19.7 0.6 gather_fusion.1
  20.3 0.1 copy.9
  20.4 0.6 gather_fusion.2
  21.0 0.1 copy.10
  21.1 0.6 gather_fusion.3
  21.6 3.4 %psum.15 = f32[32,16]{1,0:T(8,128)S(1)} all-reduce(f32[32,16]{1,0:T(8,128)S(1)} %get-tuple-element.6), channel_id=1, replica_groups=mesh['slab'=2,'bx'=8,'by'=2] {'by'}, use_global_device_ids=true, to_apply=%region_3.4 | all-reduce | flops 512 | bytes 4096 | tf_op jit(solution)/shard_map/psum | solution.py:62
  25.0 0.1 subtract_multiply_fusion.1
  25.1 0.0 collective-permute-done
  25.1 0.1 copy.13
  25.2 0.1 copy.14
  25.4 0.5 pad_maximum_fusion
  25.9 1.7 %copy-done.3 = f32[32,18,1024]{2,1,0:T(8,128)} copy-done((f32[32,18,1024]{2,1,0:T(8,128)}, f32[32,18,1024]{2,1,0:T(8,128)S(1)}, u32[]{:S(2)}) %copy-start.3) | copy-done | bytes 2359320
  27.6 1.0 fusion.9
  28.6 2.3 %collective-permute-start.2 = (f32[32,18,1]{2,1,0:T(8,128)}, f32[32,18,1]{2,1,0:T(8,128)S(1)}, u32[]{:S(2)}, u32[]{:S(2)}) collective-permute-start(f32[32,18,1]{2,1,0:T(8,128)} %get-tuple-element.12), channel_id=1, source_target_pairs={{0,1},{2,3},{4,5},{6,7},{8,9},{10,11},{12,13},{14,15},{16,17},{18,... | collective-permute-start | bytes 6920 | tf_op jit(solution)/shard_map/ppermute | solution.py:18
  30.8 1.3 %collective-permute-start.3 = (f32[32,18,1]{2,1,0:T(8,128)}, f32[32,18,1]{2,1,0:T(8,128)}, u32[]{:S(2)}, u32[]{:S(2)}) collective-permute-start(f32[32,18,1]{2,1,0:T(8,128)} %get-tuple-element.11), channel_id=1, source_target_pairs={{1,0},{3,2},{5,4},{7,6},{9,8},{11,10},{13,12},{15,14},{17,16},{19,... | collective-permute-start | bytes 6920 | tf_op jit(solution)/shard_map/ppermute | solution.py:20
  32.1 58.6 %all-reduce.3.cloned.1.call-done = f32[32,1024]{1,0:T(8,128)} async-done(((f32[32,1024]{1,0:T(8,128)}), f32[32,1024]{1,0:T(8,128)}) %all-reduce.3.cloned.1.call-update) | async-done | bytes 131088 | tf_op jit(solution)/shard_map/psum | solution.py:64
  90.8 1.0 subtract_multiply_fusion
  91.8 0.0 collective-permute-done.2
  91.8 0.0 collective-permute-done.3
  91.8 4.8 %concatenate.7 = f32[32,18,1026]{2,1,0:T(8,128)} concatenate(f32[32,18,1]{2,1,0:T(8,128)S(1)} %collective-permute-done.2, f32[32,18,1024]{2,1,0:T(8,128)} %copy-done.3, f32[32,18,1]{2,1,0:T(8,128)} %collective-permute-done.3), dimensions={2} | concatenate | bytes 4727808 | tf_op jit(solution)/shard_map/concatenate | solution.py:16
  96.6 11.4 %fusion.6 = (f32[33,17,1025]{2,1,0:T(8,128)S(1)}, f32[33,17,1025]{2,1,0:T(8,128)S(1)}) fusion(f32[32,18,1026]{2,1,0:T(8,128)} %concatenate.7), kind=kLoop, calls=%fused_computation.20 | loop fusion | flops 6325275 | bytes 6964104 | tf_op jit(solution)/shard_map/div | solution.py:33
  108.1 1.5 %fusion.7 = (f32[33,17,1025]{2,1,0:T(8,128)S(1)}, f32[33,17,1025]{2,1,0:T(8,128)S(1)}) fusion(f32[33,17,1025]{2,1,0:T(8,128)S(1)} %get-tuple-element.8, f32[32,18,1026]{2,1,0:T(8,128)S(1)} %copy-done.1), kind=kLoop, calls=%fused_computation.21 | loop fusion | flops 2300100 | bytes 9264204 | tf_op jit(solution)/shard_map/div | solution.py:34
  109.6 4.9 %fusion.2 = f32[32,16,1024]{2,1,0:T(8,128)} fusion(f32[33,17,1025]{2,1,0:T(8,128)S(1)} %get-tuple-element.10, f32[33,17,1025]{2,1,0:T(8,128)S(1)} %get-tuple-element.9, f32[33,17,1025]{2,1,0:T(8,128)S(1)} %get-tuple-element.7, f32[32,16,1024]{2,1,0:T(8,128)S(1)} %copy-done.2, f32[32,16]{1,0:T(8,128)S(1)} %subtract_multiply_fusion.1, ...), kind=kLoop, calls=%fused_computation.13 | loop fusion | flops 6291456 | bytes 16910336 | tf_op jit(solution)/shard_map/sub | solution.py:69
  (17 shorter events, 0.1 us)
Async XLA Ops:
  6.5 12.5 %copy-start = (s32[64,1024]{1,0:T(8,128)S(1)}, s32[64,1024]{1,0:T(8,128)}, u32[]{:S(2)}) copy-start(s32[64,1024]{1,0:T(8,128)} %param.9) | copy-start | bytes 786436
  6.5 18.8 %copy-start.2 = (f32[32,16,1024]{2,1,0:T(8,128)S(1)}, f32[32,16,1024]{2,1,0:T(8,128)}, u32[]{:S(2)}) copy-start(f32[32,16,1024]{2,1,0:T(8,128)} %param.6) | copy-start | bytes 6291460
  6.5 13.1 %copy-start.4 = (f32[64,1024]{1,0:T(8,128)S(1)}, f32[64,1024]{1,0:T(8,128)}, u32[]{:S(2)}) copy-start(f32[64,1024]{1,0:T(8,128)} %param.7) | copy-start | bytes 786436
  6.5 13.8 %copy-start.5 = (s32[64,16]{0,1:T(8,128)S(1)}, s32[64,16]{0,1:T(8,128)}, u32[]{:S(2)}) copy-start(s32[64,16]{0,1:T(8,128)} %param.10) | copy-start | bytes 12292
  6.5 14.4 %copy-start.6 = (f32[64,16]{0,1:T(8,128)S(1)}, f32[64,16]{0,1:T(8,128)}, u32[]{:S(2)}) copy-start(f32[64,16]{0,1:T(8,128)} %param.8) | copy-start | bytes 12292
  6.5 84.2 %all-reduce.3.cloned.1.call-start = ((), (), s32[]{:S(2)}) async-start(), calls=%async_computation | async-start | bytes 262144 | tf_op jit(solution)/shard_map/psum | solution.py:64
  8.5 16.5 %collective-permute-start = (f32[32,1,1024]{2,0,1:T(8,128)S(1)}, f32[32,1,1024]{2,0,1:T(8,128)S(1)}, u32[]{:S(2)}, u32[]{:S(2)}) collective-permute-start(f32[32,1,1024]{2,0,1:T(8,128)S(1)} %copy.15), channel_id=1, source_target_pairs={{0,2},{2,4},{4,6},{6,8},{8,10},{10,12},{12,14},{1,3},{3,5},{5,7},{... | collective-permute-start | bytes 393224 | tf_op jit(solution)/shard_map/ppermute | solution.py:18
  13.5 11.7 %collective-permute-start.1 = (f32[32,1,1024]{2,0,1:T(8,128)S(1)}, f32[32,1,1024]{2,0,1:T(8,128)S(1)}, u32[]{:S(2)}, u32[]{:S(2)}) collective-permute-start(f32[32,1,1024]{2,0,1:T(8,128)S(1)} %copy.16), channel_id=1, source_target_pairs={{2,0},{4,2},{6,4},{8,6},{10,8},{12,10},{14,12},{3,1},{5,3},{7,5},{... | collective-permute-start | bytes 393224 | tf_op jit(solution)/shard_map/ppermute | solution.py:20
  25.9 1.7 %copy-start.3 = (f32[32,18,1024]{2,1,0:T(8,128)}, f32[32,18,1024]{2,1,0:T(8,128)S(1)}, u32[]{:S(2)}) copy-start(f32[32,18,1024]{2,1,0:T(8,128)S(1)} %pad_maximum_fusion) | copy-start | bytes 7077892
  28.6 63.2 %collective-permute-start.2 = (f32[32,18,1]{2,1,0:T(8,128)}, f32[32,18,1]{2,1,0:T(8,128)S(1)}, u32[]{:S(2)}, u32[]{:S(2)}) collective-permute-start(f32[32,18,1]{2,1,0:T(8,128)} %get-tuple-element.12), channel_id=1, source_target_pairs={{0,1},{2,3},{4,5},{6,7},{8,9},{10,11},{12,13},{14,15},{16,17},{18,... | collective-permute-start | bytes 6920 | tf_op jit(solution)/shard_map/ppermute | solution.py:18
  30.8 60.9 %collective-permute-start.3 = (f32[32,18,1]{2,1,0:T(8,128)}, f32[32,18,1]{2,1,0:T(8,128)}, u32[]{:S(2)}, u32[]{:S(2)}) collective-permute-start(f32[32,18,1]{2,1,0:T(8,128)} %get-tuple-element.11), channel_id=1, source_target_pairs={{1,0},{3,2},{5,4},{7,6},{9,8},{11,10},{13,12},{15,14},{17,16},{19,... | collective-permute-start | bytes 6920 | tf_op jit(solution)/shard_map/ppermute | solution.py:20
  96.6 11.4 %copy-start.1 = (f32[32,18,1026]{2,1,0:T(8,128)S(1)}, f32[32,18,1026]{2,1,0:T(8,128)}, u32[]{:S(2)}) copy-start(f32[32,18,1026]{2,1,0:T(8,128)} %concatenate.7) | copy-start | bytes 7091716
Sparse Core Ops, SparseCore 0:
  17.8 72.8 all-reduce.2
where the time goes:
time: 122 us; the launch traced here: 121 us
  waiting for transfers between devices  58.7 us (48%)
  other arithmetic  23.7 us (19%)
  between operations  13.6 us (11%)
  local copies, waits for them, and re-layouts  12.3 us (10%)
  starting transfers between devices  9.76 us (8%)
  blocking collectives  3.36 us (3%)
    psum x1, waiting for transfers between devices, per_device(): first_projection = lax.psum(part_a, 'bx') * (4.0 / total_x)  58.6 us
    div x1, other arithmetic, curvature_of(): flux_z = grad_z / magnitude  11.4 us
    ppermute x2, starting transfers between devices, extended(): lax.ppermute(tail, axis, [(i, (i + 1) % count) for i in range(ends)])  7.14 us
    sub x1, other arithmetic, per_device(): slope * (first_residual[:, None, :] + second_residual[:, :, None])  4.89 us
    concatenate x1, local copies, waits for them, and re-layouts, extended(): jnp.concatenate([lax.ppermute(tail, axis, [(i, (i + 1) % count) for i in...  4.83 us
    psum x1, blocking collectives, per_device(): second_projection = lax.psum(part_b, 'by') * (4.0 / total_y)  3.36 us
    reduce_sum x1, other arithmetic, per_device(): part_a = jnp.sum(heav, axis=1)  2.91 us
    ppermute x2, starting transfers between devices, extended(): lax.ppermute(head, axis, [((i + 1) % count, i) for i in range(ends)])  2.58 us
  transfers between devices with their start and end apart: 5, of which 1 were waited for; matrix products, arithmetic and copies ran while one was open for 8% of the time, Pallas kernels for 0%

commit v1 on v0

--- a/solution.py
+++ b/solution.py
@@ -5,6 +5,10 @@
 
 LAMBDA = 0.5
 BETA2 = 1.0
+
+
+def place_state(my_data):
+    return lax.all_gather(my_data, "bx").sum(axis=0)
 
 
 def extended(cells, sides, width):
@@ -61,7 +65,7 @@
     second_mask_rows = jnp.take(second_view_mask, plane_detector_rows, axis=0).astype(jnp.float32)
     second_projection = lax.psum(part_b, "by") * (4.0 / total_y)
     second_residual = second_mask_rows * (second_projection - second_measured_rows)
-    first_projection = lax.psum(part_a, "bx") * (4.0 / total_x)
+    first_projection = place_state(part_a) * (4.0 / total_x)
     first_residual = first_mask_rows * (first_projection - first_measured_rows)
     padded = extended(phi, (("bx", 1), ("by", 2)), 1)
     padded = jnp.pad(padded, ((1, 1), (0, 0), (0, 0)))

time: 122 us -> 79 us (0.65)
  waiting for transfers between devices: 58.7 us -> 6.31 us
  other arithmetic: 23.7 us -> 31.9 us
  local copies, waits for them, and re-layouts: 12.3 us -> 13.7 us
    psum x1 -> x0, waiting for transfers between devices: 58.6 us -> none  [per_device(): first_projection = lax.psum(part_a, 'bx') * (4.0 / total_x)]
    all_gather x0 -> x1, waiting for transfers between devices: none -> 4.96 us  [place_state(): return lax.all_gather(my_data, 'bx').sum(axis=0)]
    sub x1, other arithmetic: 4.89 us -> 9.85 us  [per_device(): slope * (first_residual[:, None, :] + second_residual[:, :, None])]
    div x1, other arithmetic: 1.54 us -> 3.78 us  [curvature_of(): flux_x = grad_x / magnitude]
    unnamed x18 -> x16, local copies, waits for them, and re-layouts: 1.92 us -> 3.26 us
    ppermute x2, waiting for transfers between devices: 0.01 us -> 1.32 us  [extended(): lax.ppermute(head, axis, [((i + 1) % count, i) for i in range(ends)])]
    reduce_sum x0 -> x1, other arithmetic: none -> 1.29 us  [place_state(): return lax.all_gather(my_data, 'bx').sum(axis=0)]
    div x1, other arithmetic: 11.4 us -> 12.7 us  [curvature_of(): flux_z = grad_z / magnitude]
  transfers between devices with their start and end apart: 5 -> 5, of which waited for: 1 -> 2; matrix products, arithmetic and copies ran while one was open for 8% -> 39% of each run, Pallas kernels for 0% -> 0%
where the time goes in v1:
time: 79 us; the launch traced here: 78.6 us
  other arithmetic  31.9 us (40%)
  local copies, waits for them, and re-layouts  13.7 us (17%)
  between operations  13.6 us (17%)
  starting transfers between devices  9.72 us (12%)
  waiting for transfers between devices  6.31 us (8%)
  blocking collectives  3.36 us (4%)
    div x1, other arithmetic, curvature_of(): flux_z = grad_z / magnitude  12.7 us
    sub x1, other arithmetic, per_device(): slope * (first_residual[:, None, :] + second_residual[:, :, None])  9.85 us
    ppermute x2, starting transfers between devices, extended(): lax.ppermute(tail, axis, [(i, (i + 1) % count) for i in range(ends)])  7.13 us
    all_gather x1, waiting for transfers between devices, place_state(): return lax.all_gather(my_data, 'bx').sum(axis=0)  4.96 us
    concatenate x1, local copies, waits for them, and re-layouts, extended(): jnp.concatenate([lax.ppermute(tail, axis, [(i, (i + 1) % count) for i in...  4.89 us
    div x1, other arithmetic, curvature_of(): flux_x = grad_x / magnitude  3.78 us
    psum x1, blocking collectives, per_device(): second_projection = lax.psum(part_b, 'by') * (4.0 / total_y)  3.36 us
    unnamed x16, local copies, waits for them, and re-layouts  3.26 us
  transfers between devices with their start and end apart: 5, of which 2 were waited for; matrix products, arithmetic and copies ran while one was open for 39% of the time, Pallas kernels for 0%

profile of v1, /device:TPU:0, one launch (start us, length us, event | category | flops | bytes accessed | tf_op | source)
XLA Modules:
  0.0 78.6 jit_solution(5808721985318435154)
XLA Ops:
  6.5 1.9 %fusion.10 = (f32[32,1,1024]{2,1,0:T(1,128)S(1)}, f32[32,1,1024]{2,1,0:T(1,128)S(1)}) fusion(f32[32,16,1024]{2,1,0:T(8,128)} %param.6), kind=kLoop, calls=%fused_computation.29 | loop fusion | bytes 524288 | tf_op jit(solution)/shard_map/slice | solution.py:19
  8.5 4.9 %collective-permute-start = (f32[32,1,1024]{2,0,1:T(8,128)S(1)}, f32[32,1,1024]{2,0,1:T(8,128)S(1)}, u32[]{:S(2)}, u32[]{:S(2)}) collective-permute-start(f32[32,1,1024]{2,0,1:T(8,128)S(1)} %copy.21), channel_id=1, source_target_pairs={{0,2},{2,4},{4,6},{6,8},{8,10},{10,12},{12,14},{1,3},{3,5},{5,7},{... | collective-permute-start | bytes 393224 | tf_op jit(solution)/shard_map/ppermute | solution.py:22
  13.4 1.3 %collective-permute-start.1 = (f32[32,1,1024]{2,0,1:T(8,128)S(1)}, f32[32,1,1024]{2,0,1:T(8,128)S(1)}, u32[]{:S(2)}, u32[]{:S(2)}) collective-permute-start(f32[32,1,1024]{2,0,1:T(8,128)S(1)} %copy.22), channel_id=1, source_target_pairs={{2,0},{4,2},{6,4},{8,6},{10,8},{12,10},{14,12},{3,1},{5,3},{7,5},{... | collective-permute-start | bytes 393224 | tf_op jit(solution)/shard_map/ppermute | solution.py:24
  14.7 2.9 %fusion.5 = (f32[32,1024]{1,0:T(8,128)}, f32[32,16]{1,0:T(8,128)S(1)}) fusion(f32[32,16,1024]{2,1,0:T(8,128)} %param.6), kind=kLoop, calls=%fused_computation.19 | loop fusion | flops 2063872 | bytes 2230272 | tf_op jit(solution)/shard_map/reduce_sum | solution.py:60
  17.6 0.0 all-gather.3.cloned.1.call-update
  17.7 0.7 compare_select_fusion
  18.3 0.8 copy.15
  19.1 0.8 copy.16
  19.9 0.6 gather_fusion.2
  20.5 0.6 gather_fusion.3
  21.0 3.4 %psum.7 = f32[32,16]{1,0:T(8,128)S(1)} all-reduce(f32[32,16]{1,0:T(8,128)S(1)} %get-tuple-element.6), channel_id=1, replica_groups=mesh['slab'=2,'bx'=8,'by'=2] {'by'}, use_global_device_ids=true, to_apply=%region_3.4 | all-reduce | flops 512 | bytes 4096 | tf_op jit(solution)/shard_map/psum | solution.py:66
  24.4 0.0 collective-permute-done
  24.4 0.1 copy.19
  24.6 0.1 copy.20
  24.7 0.0 copy-start.4
  24.8 0.5 pad_maximum_fusion
  25.3 1.6 %copy-done.3 = f32[32,18,1024]{2,1,0:T(8,128)} copy-done((f32[32,18,1024]{2,1,0:T(8,128)}, f32[32,18,1024]{2,1,0:T(8,128)S(1)}, u32[]{:S(2)}) %copy-start.3) | copy-done | bytes 2359320
  26.9 1.0 %fusion.9 = (f32[32,18,1]{2,1,0:T(8,128)}, f32[32,18,1]{2,1,0:T(8,128)}) fusion(f32[32,18,1024]{2,1,0:T(8,128)S(1)} %pad_maximum_fusion), kind=kLoop, calls=%fused_computation.28 | loop fusion | bytes 9216 | tf_op jit(solution)/shard_map/slice | solution.py:18
  28.0 2.3 %collective-permute-start.2 = (f32[32,18,1]{2,1,0:T(8,128)}, f32[32,18,1]{2,1,0:T(8,128)S(1)}, u32[]{:S(2)}, u32[]{:S(2)}) collective-permute-start(f32[32,18,1]{2,1,0:T(8,128)} %get-tuple-element.12), channel_id=1, source_target_pairs={{0,1},{2,3},{4,5},{6,7},{8,9},{10,11},{12,13},{14,15},{16,17},{18,... | collective-permute-start | bytes 6920 | tf_op jit(solution)/shard_map/ppermute | solution.py:22
  30.2 1.3 %collective-permute-start.3 = (f32[32,18,1]{2,1,0:T(8,128)}, f32[32,18,1]{2,1,0:T(8,128)}, u32[]{:S(2)}, u32[]{:S(2)}) collective-permute-start(f32[32,18,1]{2,1,0:T(8,128)} %get-tuple-element.11), channel_id=1, source_target_pairs={{1,0},{3,2},{5,4},{7,6},{9,8},{11,10},{13,12},{15,14},{17,16},{19,... | collective-permute-start | bytes 6920 | tf_op jit(solution)/shard_map/ppermute | solution.py:24
  31.5 0.1 subtract_multiply_fusion.1
  31.6 0.6 gather_fusion
  32.2 0.6 gather_fusion.1
  32.8 0.0 collective-permute-done.2
  32.9 1.3 %collective-permute-done.3 = f32[32,18,1]{2,1,0:T(8,128)} collective-permute-done((f32[32,18,1]{2,1,0:T(8,128)}, f32[32,18,1]{2,1,0:T(8,128)}, u32[]{:S(2)}, u32[]{:S(2)}) %collective-permute-start.3) | collective-permute-done | bytes 2336 | tf_op jit(solution)/shard_map/ppermute | solution.py:24
  34.2 4.9 %concatenate.7 = f32[32,18,1026]{2,1,0:T(8,128)} concatenate(f32[32,18,1]{2,1,0:T(8,128)S(1)} %collective-permute-done.2, f32[32,18,1024]{2,1,0:T(8,128)} %copy-done.3, f32[32,18,1]{2,1,0:T(8,128)} %collective-permute-done.3), dimensions={2} | concatenate | bytes 4727808 | tf_op jit(solution)/shard_map/concatenate | solution.py:20
  39.1 12.7 %fusion.6 = (f32[33,17,1025]{2,1,0:T(8,128)}, f32[33,17,1025]{2,1,0:T(8,128)S(1)}) fusion(f32[32,18,1026]{2,1,0:T(8,128)} %concatenate.7), kind=kLoop, calls=%fused_computation.20 | loop fusion | flops 6325275 | bytes 6964104 | tf_op jit(solution)/shard_map/div | solution.py:37
  51.8 3.8 %fusion.7 = (f32[33,17,1025]{2,1,0:T(8,128)}, f32[33,17,1025]{2,1,0:T(8,128)}) fusion(f32[33,17,1025]{2,1,0:T(8,128)S(1)} %get-tuple-element.8, f32[32,18,1026]{2,1,0:T(8,128)S(1)} %copy-done.1), kind=kLoop, calls=%fused_computation.21 | loop fusion | flops 2300100 | bytes 9264204 | tf_op jit(solution)/shard_map/div | solution.py:38
  55.5 5.0 %all-gather.3.cloned.1.call-done = f32[256,1024]{1,0:T(8,128)} async-done(((f32[32,1024]{1,0:T(8,128)}), f32[256,1024]{1,0:T(8,128)}) %all-gather.3.cloned.1.call-update) | async-done | bytes 1048592 | tf_op jit(solution)/shard_map/all_gather | solution.py:11
  60.5 1.3 %reduce_sum.28 = f32[32,1024]{1,0:T(8,128)S(1)} reduce(f32[8,32,1024]{2,1,0:T(8,128)} %bitcast.1, f32[]{:T(128)} %constant.62.clone.1), dimensions={0}, to_apply=%region_1.0 | reduce | flops 229376 | bytes 1179652 | tf_op jit(solution)/shard_map/reduce_sum | solution.py:11
  61.8 0.1 subtract_multiply_fusion
  61.9 9.8 %fusion.2 = f32[32,16,1024]{2,1,0:T(8,128)} fusion(f32[33,17,1025]{2,1,0:T(8,128)} %get-tuple-element.10, f32[33,17,1025]{2,1,0:T(8,128)} %get-tuple-element.9, f32[33,17,1025]{2,1,0:T(8,128)} %get-tuple-element.7, f32[32,16,1024]{2,1,0:T(8,128)S(1)} %copy-done.2, f32[32,16]{1,0:T(8,128)S(1)} %subtract_multiply_fusion.1, f32[32,1024]{1,0:T(8,128)S(1)} %subtract_multiply_fusion), kind=kLoop, calls=%fused_computation.13 | loop fusion | flops 6291456 | bytes 16910336 | tf_op jit(solution)/shard_map/sub | solution.py:73
  (16 shorter events, 0.1 us)
Async XLA Ops:
  6.5 25.1 %copy-start = (s32[64,1024]{1,0:T(8,128)S(1)}, s32[64,1024]{1,0:T(8,128)}, u32[]{:S(2)}) copy-start(s32[64,1024]{1,0:T(8,128)} %param.9) | copy-start | bytes 786436
  6.5 18.2 %copy-start.2 = (f32[32,16,1024]{2,1,0:T(8,128)S(1)}, f32[32,16,1024]{2,1,0:T(8,128)}, u32[]{:S(2)}) copy-start(f32[32,16,1024]{2,1,0:T(8,128)} %param.6) | copy-start | bytes 6291460
  6.5 17.9 %copy-start.5 = (s32[32]{0:T(128)S(1)}, s32[32]{0:T(128)}, u32[]{:S(2)}) copy-start(s32[32]{0:T(128)} %param.11) | copy-start | bytes 388
  6.5 54.0 %all-gather.3.cloned.1.call-start = ((), (), s32[]{:S(2)}) async-start(), calls=%async_computation | async-start | bytes 1179648 | tf_op jit(solution)/shard_map/all_gather | solution.py:11
  8.5 15.9 %collective-permute-start = (f32[32,1,1024]{2,0,1:T(8,128)S(1)}, f32[32,1,1024]{2,0,1:T(8,128)S(1)}, u32[]{:S(2)}, u32[]{:S(2)}) collective-permute-start(f32[32,1,1024]{2,0,1:T(8,128)S(1)} %copy.21), channel_id=1, source_target_pairs={{0,2},{2,4},{4,6},{6,8},{8,10},{10,12},{12,14},{1,3},{3,5},{5,7},{... | collective-permute-start | bytes 393224 | tf_op jit(solution)/shard_map/ppermute | solution.py:22
  13.4 11.2 %collective-permute-start.1 = (f32[32,1,1024]{2,0,1:T(8,128)S(1)}, f32[32,1,1024]{2,0,1:T(8,128)S(1)}, u32[]{:S(2)}, u32[]{:S(2)}) collective-permute-start(f32[32,1,1024]{2,0,1:T(8,128)S(1)} %copy.22), channel_id=1, source_target_pairs={{2,0},{4,2},{6,4},{8,6},{10,8},{12,10},{14,12},{3,1},{5,3},{7,5},{... | collective-permute-start | bytes 393224 | tf_op jit(solution)/shard_map/ppermute | solution.py:24
  24.7 7.5 %copy-start.4 = (f32[64,1024]{1,0:T(8,128)S(1)}, f32[64,1024]{1,0:T(8,128)}, u32[]{:S(2)}) copy-start(f32[64,1024]{1,0:T(8,128)} %param.7) | copy-start | bytes 786436
  25.3 1.6 %copy-start.3 = (f32[32,18,1024]{2,1,0:T(8,128)}, f32[32,18,1024]{2,1,0:T(8,128)S(1)}, u32[]{:S(2)}) copy-start(f32[32,18,1024]{2,1,0:T(8,128)S(1)} %pad_maximum_fusion) | copy-start | bytes 7077892
  28.0 4.9 %collective-permute-start.2 = (f32[32,18,1]{2,1,0:T(8,128)}, f32[32,18,1]{2,1,0:T(8,128)S(1)}, u32[]{:S(2)}, u32[]{:S(2)}) collective-permute-start(f32[32,18,1]{2,1,0:T(8,128)} %get-tuple-element.12), channel_id=1, source_target_pairs={{0,1},{2,3},{4,5},{6,7},{8,9},{10,11},{12,13},{14,15},{16,17},{18,... | collective-permute-start | bytes 6920 | tf_op jit(solution)/shard_map/ppermute | solution.py:22
  30.2 4.0 %collective-permute-start.3 = (f32[32,18,1]{2,1,0:T(8,128)}, f32[32,18,1]{2,1,0:T(8,128)}, u32[]{:S(2)}, u32[]{:S(2)}) collective-permute-start(f32[32,18,1]{2,1,0:T(8,128)} %get-tuple-element.11), channel_id=1, source_target_pairs={{1,0},{3,2},{5,4},{7,6},{9,8},{11,10},{13,12},{15,14},{17,16},{19,... | collective-permute-start | bytes 6920 | tf_op jit(solution)/shard_map/ppermute | solution.py:24
  39.1 12.7 %copy-start.1 = (f32[32,18,1026]{2,1,0:T(8,128)S(1)}, f32[32,18,1026]{2,1,0:T(8,128)}, u32[]{:S(2)}) copy-start(f32[32,18,1026]{2,1,0:T(8,128)} %concatenate.7) | copy-start | bytes 7091716
Sparse Core Ops, SparseCore 0:
  17.8 42.6 all-gather.2
